TPU v7x, 32 devices: a whole 2x2x4 slice. The times are simulated.
32 devices in a mesh: lag: 4 (over y, x), row: 8 (over z, core).
Axes of the slice: x: 2, y: 2, z: 4, core: 2. Of those that a mesh axis runs over, the one named last changes fastest.
Arguments:
- lag_weights: float32 [16, 4096, 4096], P('lag', 'row'), may hold values from -0.0234375 to 0.0234375
- inverse_head: float32 [4096, 4096], P('row'), may hold values from -0.09375 to 0.09375
- excitation: float32 [3, 4096, 128], P(None, 'row'), may hold values from -6 to 6
- history: float32 [16, 4096, 128], P('lag', 'row'), may hold values from -6 to 6
Outputs:
- densities: float32 [3, 4096, 128], P(None, 'row')
All inputs are finite; a program needn't handle non-finite values.
Results may differ from a plain program's by a relative error of at most 0.0001.
Values sent between devices are 32-bit elements; how exact they have to be, the bound alone decides.
No kernel may reach another device: no remote copies, remote signals or barrier semaphores. Data moves between devices by JAX's collectives and lax.ppermute only.
A program may use at most 128 MiB of HBM per device.

v0:
```python
import jax
import jax.numpy as jnp
from jax import lax
from jax.sharding import PartitionSpec as P

STEPS = 3


def from_behind(value, axis, steps):
    count = lax.axis_size(axis)
    leading, last = (max(0, -steps), min(count, count - steps))
    return lax.ppermute(value, axis, [(source, source + steps) for source in range(leading, last)])


def lag_products(weights, piece):
    return jnp.einsum("kmc,kcr->mr", weights, piece, precision=lax.Precision.HIGHEST)


def on_device(lag_weights, inverse_head, excitation, history):
    at_head = lax.axis_index("lag") == 0
    past = lax.all_gather(history, "row", axis=1, tiled=True)
    results = []
    for step in range(STEPS):
        carried = lag_products(lag_weights, past)
        carried = lax.psum(carried, "lag")
        right_side = excitation[step] - carried
        density = jnp.dot(
            inverse_head,
            lax.all_gather(right_side, "row", axis=0, tiled=True),
            precision=lax.Precision.HIGHEST,
            preferred_element_type=jnp.float32,
        )
        results.append(density)
        if step + 1 < STEPS:
            whole_density = lax.all_gather(density, "row", axis=0, tiled=True)
            moved = from_behind(past[-1], "lag", 1)
            entering = jnp.where(at_head, whole_density, moved)
            past = jnp.concatenate([entering[None], past[:-1]], axis=0)
    return jnp.stack(results, axis=0)


def solution(mesh):
    placed = (P("lag", "row", None), P("row", None), P(None, "row", None), P("lag", "row", None))
    return jax.shard_map(
        on_device, mesh=mesh, in_specs=placed, out_specs=P(None, "row", None), check_vma=False
    )
```

profile of v0, /device:TPU:0, one launch (start us, length us, event | category | flops | bytes accessed | tf_op | source)
XLA Modules:
  0.0 563.5 jit_solution(13473457763976468164)
XLA Ops:
  6.5 0.0 all-gather.7.cloned.1.call-start
  6.5 2.6 copy.5
  9.2 0.0 all-gather.7.cloned.1.call-update
  9.2 0.0 copy-start.4
  9.2 0.0 all-reduce.4.cloned.1.call-start
  9.3 84.8 %all-gather.7.cloned.1.call-done = f32[4,4096,128]{1,2,0:T(8,128)} async-done(((f32[4,512,128]{1,2,0:T(8,128)}), f32[4,4096,128]{1,2,0:T(8,128)}) %all-gather.7.cloned.1.call-update) | async-done | bytes 8388624 | tf_op jit(solution)/shard_map/all_gather | solution.py:21
  94.1 31.3 %convolution_bitcast_fusion.1 = f32[512,128]{1,0:T(8,128)} fusion(f32[4,512,4096]{2,1,0:T(8,128)} %param.4, f32[4,4096,128]{1,2,0:T(8,128)} %all-gather.7.cloned.1.call-done), kind=kOutput, calls=%fused_computation.16 | convolution fusion | flops 12884901888 | bytes 42205184 | tf_op jit(solution)/shard_map/kmc,kcr->mr/dot_general | solution.py:16
  125.4 0.0 all-reduce.4.cloned.1.call-update
  125.5 0.0 all-gather.9.cloned.1.call-start
  125.5 41.6 %all-reduce.4.cloned.1.call-done = f32[512,128]{1,0:T(8,128)} async-done(((f32[512,128]{1,0:T(8,128)}), f32[512,128]{1,0:T(8,128)}) %all-reduce.4.cloned.1.call-update) | async-done | bytes 262160 | tf_op jit(solution)/shard_map/psum | solution.py:25
  167.1 1.7 bitcast_subtract_fusion.2
  168.8 0.0 all-gather.9.cloned.1.call-update
  168.8 0.3 all-gather.11.cloned.1.call-start
  169.2 29.0 %all-gather.9.cloned.1.call-done = f32[4096,128]{1,0:T(8,128)} async-done(((f32[512,128]{1,0:T(8,128)}), f32[4096,128]{1,0:T(8,128)}) %all-gather.9.cloned.1.call-update) | async-done | bytes 2097168 | tf_op jit(solution)/shard_map/all_gather | solution.py:29
  198.1 13.5 %fusion.17 = f32[128,512]{1,0:T(8,128)} fusion(f32[4096,128]{1,0:T(8,128)} %all-gather.9.cloned.1.call-done, f32[512,4096]{1,0:T(8,128)} %param.5), kind=kOutput, calls=%fused_computation.23 | convolution fusion | flops 3221225472 | bytes 10747904 | tf_op jit(solution)/shard_map/dot_general | solution.py:27
  211.7 0.0 all-gather.11.cloned.1.call-update
  211.7 0.0 all-reduce.6.cloned.1.call-start
  211.7 4.7 slice_bitcast_fusion
  216.4 4.0 collective-permute-start
  220.4 6.2 %slice.30 = f32[3,4096,128]{1,2,0:T(8,128)} slice(f32[4,4096,128]{1,2,0:T(8,128)} %all-gather.7.cloned.1.call-done), slice={[0:3], [0:4096], [0:128]} | slice | bytes 12582912 | tf_op jit(solution)/shard_map/slice | solution.py:38
  226.6 38.7 %collective-permute-done = f32[4096,128]{0,1:T(8,128)S(1)} collective-permute-done((f32[4096,128]{0,1:T(8,128)}, f32[4096,128]{0,1:T(8,128)S(1)}, u32[]{:S(2)}, u32[]{:S(2)}) %collective-permute-start) | collective-permute-done | bytes 2097184 | tf_op jit(solution)/shard_map/ppermute | solution.py:12
  265.3 1.3 copy-done.3
  266.7 2.0 select_bitcast_fusion.1
  268.6 1.4 copy-done
  270.1 30.9 %fusion.12 = f32[512,128]{1,0:T(8,128)} fusion(f32[4,512,4096]{2,1,0:T(8,128)} %param.4, f32[3,4096,128]{1,2,0:T(8,128)S(1)} %copy-done, f32[1,4096,128]{1,2,0:T(8,128)S(1)} %select_bitcast_fusion.1), kind=kOutput, calls=%fused_computation.15 | convolution fusion | flops 12886999040 | bytes 42205184 | tf_op jit(solution)/shard_map/kmc,kcr->mr/dot_general | solution.py:16
  301.0 0.0 all-reduce.6.cloned.1.call-update
  301.0 0.0 all-gather.13.cloned.1.call-start
  301.0 43.5 %all-reduce.6.cloned.1.call-done = f32[512,128]{1,0:T(8,128)} async-done(((f32[512,128]{1,0:T(8,128)}), f32[512,128]{1,0:T(8,128)}) %all-reduce.6.cloned.1.call-update) | async-done | bytes 262160 | tf_op jit(solution)/shard_map/psum | solution.py:25
  344.5 1.7 bitcast_subtract_fusion.1
  346.2 0.0 all-gather.13.cloned.1.call-update
  346.2 0.2 all-gather.15.cloned.1.call-start
  346.4 29.1 %all-gather.13.cloned.1.call-done = f32[4096,128]{1,0:T(8,128)} async-done(((f32[512,128]{1,0:T(8,128)}), f32[4096,128]{1,0:T(8,128)}) %all-gather.13.cloned.1.call-update) | async-done | bytes 2097168 | tf_op jit(solution)/shard_map/all_gather | solution.py:29
  375.5 13.5 %fusion.18 = f32[128,512]{1,0:T(8,128)} fusion(f32[4096,128]{1,0:T(8,128)} %all-gather.13.cloned.1.call-done, f32[512,4096]{1,0:T(8,128)} %param.5), kind=kOutput, calls=%fused_computation.24 | convolution fusion | flops 3221225472 | bytes 10747904 | tf_op jit(solution)/shard_map/dot_general | solution.py:27
  389.0 0.0 all-gather.15.cloned.1.call-update
  389.1 0.0 all-reduce.8.cloned.1.call-start
  389.1 4.9 collective-permute-start.1
  394.0 44.1 %collective-permute-done.1 = f32[4096,128]{0,1:T(8,128)} collective-permute-done((f32[4096,128]{0,1:T(8,128)}, f32[4096,128]{0,1:T(8,128)}, u32[]{:S(2)}, u32[]{:S(2)}) %collective-permute-start.1) | collective-permute-done | bytes 2097184 | tf_op jit(solution)/shard_map/ppermute | solution.py:12
  438.1 1.8 select_bitcast_fusion
  439.9 31.1 %fusion.9 = f32[512,128]{1,0:T(8,128)} fusion(f32[4,512,4096]{2,1,0:T(8,128)} %param.4, f32[3,4096,128]{1,2,0:T(8,128)} %slice.30, f32[1,4096,128]{1,2,0:T(8,128)S(1)} %select_bitcast_fusion.1, f32[1,4096,128]{1,2,0:T(8,128)S(1)} %select_bitcast_fusion), kind=kOutput, calls=%fused_computation.13 | convolution fusion | flops 12889096192 | bytes 44302336 | tf_op jit(solution)/shard_map/kmc,kcr->mr/dot_general | solution.py:16
  471.0 0.0 all-reduce.8.cloned.1.call-update
  471.0 0.0 all-gather.17.cloned.1.call-start
  471.1 43.6 %all-reduce.8.cloned.1.call-done = f32[512,128]{1,0:T(8,128)} async-done(((f32[512,128]{1,0:T(8,128)}), f32[512,128]{1,0:T(8,128)}) %all-reduce.8.cloned.1.call-update) | async-done | bytes 262160 | tf_op jit(solution)/shard_map/psum | solution.py:25
  514.6 1.7 bitcast_subtract_fusion
  516.3 0.0 all-gather.17.cloned.1.call-update
  516.4 29.3 %all-gather.17.cloned.1.call-done = f32[4096,128]{1,0:T(8,128)} async-done(((f32[512,128]{1,0:T(8,128)}), f32[4096,128]{1,0:T(8,128)}) %all-gather.17.cloned.1.call-update) | async-done | bytes 2097168 | tf_op jit(solution)/shard_map/all_gather | solution.py:29
  545.7 9.9 %convolution_bitcast_fusion = f32[1,512,128]{1,2,0:T(8,128)S(1)} fusion(f32[4096,128]{1,0:T(8,128)} %all-gather.17.cloned.1.call-done, f32[512,4096]{1,0:T(8,128)} %param.5), kind=kOutput, calls=%fused_computation.14 | convolution fusion | flops 3221225472 | bytes 10747904 | tf_op jit(solution)/shard_map/dot_general | solution.py:27
  555.6 0.1 pad_maximum_fusion.1
  555.6 1.1 copy.6
  (9 shorter events, 0.0 us)
Async XLA Ops:
  6.5 87.6 %all-gather.7.cloned.1.call-start = ((), (), s32[]{:S(2)}) async-start(), calls=%async_computation | async-start | bytes 9437184 | tf_op jit(solution)/shard_map/all_gather | solution.py:21
  9.2 157.9 %copy-start.4 = (f32[3,512,128]{2,1,0:T(8,128)S(1)}, f32[3,512,128]{2,1,0:T(8,128)}, u32[]{:S(2)}) copy-start(f32[3,512,128]{2,1,0:T(8,128)} %param.6) | copy-start | bytes 2359300
  9.2 157.9 %all-reduce.4.cloned.1.call-start = ((), (), s32[]{:S(2)}) async-start(), calls=%async_computation.1 | async-start | bytes 524288 | tf_op jit(solution)/shard_map/psum | solution.py:25
  125.5 72.7 %all-gather.9.cloned.1.call-start = ((), (), s32[]{:S(2)}) async-start(), calls=%async_computation.2 | async-start | bytes 2359296 | tf_op jit(solution)/shard_map/all_gather | solution.py:29
  168.8 97.8 %all-gather.11.cloned.1.call-start = ((), (), s32[]{:S(2)}) async-start(), calls=%async_computation.3 | async-start | bytes 2359296 | tf_op jit(solution)/shard_map/all_gather | solution.py:35
  211.7 132.8 %all-reduce.6.cloned.1.call-start = ((), (), s32[]{:S(2)}) async-start(), calls=%async_computation.4 | async-start | bytes 524288 | tf_op jit(solution)/shard_map/psum | solution.py:25
  216.4 48.9 %collective-permute-start = (f32[4096,128]{0,1:T(8,128)}, f32[4096,128]{0,1:T(8,128)S(1)}, u32[]{:S(2)}, u32[]{:S(2)}) collective-permute-start(f32[4096,128]{0,1:T(8,128)} %get-tuple-element.6), channel_id=1, source_target_pairs={{0,8},{8,16},{16,24},{1,9},{9,17},{17,25},{2,10},{10,18},{18,26},{... | collective-permute-start | bytes 6291464 | tf_op jit(solution)/shard_map/ppermute | solution.py:12
  265.3 1.3 copy-start.3
  266.7 3.4 copy-start
  301.0 74.5 %all-gather.13.cloned.1.call-start = ((), (), s32[]{:S(2)}) async-start(), calls=%async_computation.5 | async-start | bytes 2359296 | tf_op jit(solution)/shard_map/all_gather | solution.py:29
  346.2 91.9 %all-gather.15.cloned.1.call-start = ((), (), s32[]{:S(2)}) async-start(), calls=%async_computation.6 | async-start | bytes 2359296 | tf_op jit(solution)/shard_map/all_gather | solution.py:35
  389.1 125.6 %all-reduce.8.cloned.1.call-start = ((), (), s32[]{:S(2)}) async-start(), calls=%async_computation.7 | async-start | bytes 524288 | tf_op jit(solution)/shard_map/psum | solution.py:25
  389.1 49.0 %collective-permute-start.1 = (f32[4096,128]{0,1:T(8,128)}, f32[4096,128]{0,1:T(8,128)}, u32[]{:S(2)}, u32[]{:S(2)}) collective-permute-start(f32[4096,128]{0,1:T(8,128)} %get-tuple-element.5), channel_id=1, source_target_pairs={{0,8},{8,16},{16,24},{1,9},{9,17},{17,25},{2,10},{10,18},{18,26},{... | collective-permute-start | bytes 6291464 | tf_op jit(solution)/shard_map/ppermute | solution.py:12
  471.0 84.5 %copy-start.1 = (f32[128,512]{1,0:T(8,128)S(1)}, f32[128,512]{1,0:T(8,128)}, u32[]{:S(2)}) copy-start(f32[128,512]{1,0:T(8,128)} %fusion.17) | copy-start | bytes 786436
  471.0 84.5 %copy-start.2 = (f32[128,512]{1,0:T(8,128)S(1)}, f32[128,512]{1,0:T(8,128)}, u32[]{:S(2)}) copy-start(f32[128,512]{1,0:T(8,128)} %fusion.18) | copy-start | bytes 786436
  471.0 74.6 %all-gather.17.cloned.1.call-start = ((), (), s32[]{:S(2)}) async-start(), calls=%async_computation.8 | async-start | bytes 2359296 | tf_op jit(solution)/shard_map/all_gather | solution.py:29
Sparse Core Ops, SparseCore 0:
  9.3 84.7 all-gather.6
  125.6 41.5 all-reduce.3
  169.0 29.1 all-gather.8
  211.8 28.5 all-gather.10
  301.1 43.3 all-reduce.5
  346.3 29.1 all-gather.12
  389.2 28.5 all-gather.14
  471.2 43.4 all-reduce.7
  516.5 29.1 all-gather.16
where the time goes:
time: 570 us; the launch traced here: 564 us
  waiting for transfers between devices  384 us (67%)
  matrix products  130 us (23%)
  local copies, waits for them, and re-layouts  17.4 us (3%)
  between operations  13.5 us (2%)
  starting transfers between devices  9.68 us (2%)
  other arithmetic  8.88 us (2%)
    psum x3, waiting for transfers between devices, on_device(): carried = lax.psum(carried, 'lag')  129 us
    dot_general x3, matrix products, lag_products(): jnp.einsum('kmc,kcr->mr', weights, piece, precision=lax.Precision.HIGHEST)  93.3 us
    all_gather x3, waiting for transfers between devices, on_device(): lax.all_gather(right_side, 'row', axis=0, tiled=True)  87.4 us
    all_gather x1, waiting for transfers between devices, on_device(): past = lax.all_gather(history, 'row', axis=1, tiled=True)  84.8 us
    ppermute x2, waiting for transfers between devices, from_behind(): lax.ppermute(value, axis, [(source, source + steps) for source in range(l...  82.8 us
    dot_general x3, matrix products, on_device(): jnp.dot(inverse_head, lax.all_gather(right_side, 'row', axis=0, tiled=Tru...  36.9 us
  transfers between devices with their start and end apart: 11, of which 9 were waited for; matrix products, arithmetic and copies ran while one was open for 2% of the time, Pallas kernels for 0%

commit v1 on v0

--- a/solution.py
+++ b/solution.py
@@ -22,7 +22,7 @@
     results = []
     for step in range(STEPS):
         carried = lag_products(lag_weights, past)
-        carried = lax.psum(carried, "lag")
+        carried = jnp.sum(lax.all_gather(carried, "lag"), axis=0)
         right_side = excitation[step] - carried
         density = jnp.dot(
             inverse_head,

time: 570 us -> 529 us (0.928); the launches traced: 564 us -> 529 us
  waiting for transfers between devices: 384 us -> 336 us
  matrix products: 130 us -> 142 us
    psum x3 -> x0, waiting for transfers between devices: 129 us -> none  [on_device(): carried = lax.psum(carried, 'lag')]
    all_gather x0 -> x3, waiting for transfers between devices: none -> 77 us  [on_device(): carried = jnp.sum(lax.all_gather(carried, 'lag'), axis=0)]
    dot_general x3, matrix products: 93.3 us -> 112 us  [lag_products(): jnp.einsum('kmc,kcr->mr', weights, piece, precision=lax.Precision.HIGHEST)]
    dot_general x3, matrix products: 36.9 us -> 29.5 us  [on_device(): jnp.dot(inverse_head, lax.all_gather(right_side, 'row', axis=0, tiled=Tru...]
where the time goes in v1:
time: 529 us
  waiting for transfers between devices  336 us (64%)
  matrix products  142 us (27%)
  local copies, waits for them, and re-layouts  18.8 us (4%)
  between operations  13.3 us (3%)
  other arithmetic  10.4 us (2%)
  starting transfers between devices  8.95 us (2%)
    dot_general x3, matrix products, lag_products(): jnp.einsum('kmc,kcr->mr', weights, piece, precision=lax.Precision.HIGHEST)  112 us
    all_gather x3, waiting for transfers between devices, on_device(): lax.all_gather(right_side, 'row', axis=0, tiled=True)  87.8 us
    all_gather x1, waiting for transfers between devices, on_device(): past = lax.all_gather(history, 'row', axis=1, tiled=True)  86.4 us
    ppermute x2, waiting for transfers between devices, from_behind(): lax.ppermute(value, axis, [(source, source + steps) for source in range(l...  83.6 us
    all_gather x3, waiting for transfers between devices, on_device(): carried = jnp.sum(lax.all_gather(carried, 'lag'), axis=0)  77 us
    dot_general x3, matrix products, on_device(): jnp.dot(inverse_head, lax.all_gather(right_side, 'row', axis=0, tiled=Tru...  29.5 us
  transfers between devices with their start and end apart: 11, of which 9 were waited for; matrix products, arithmetic and copies ran while one was open for 2% of the time, Pallas kernels for 0%

profile of v1, /device:TPU:0, one launch (start us, length us, event | category | flops | bytes accessed | tf_op | source)
XLA Modules:
  0.0 528.9 jit_solution(16187300830743242943)
XLA Ops:
  6.5 0.7 all-gather.13.cloned.1.call-update
  7.3 0.0 all-gather.25.cloned.1.call-start
  7.3 86.4 %all-gather.13.cloned.1.call-done = f32[4,4096,128]{2,1,0:T(8,128)} async-done(((f32[4,512,128]{2,1,0:T(8,128)}), f32[4,4096,128]{2,1,0:T(8,128)}) %all-gather.13.cloned.1.call-update) | async-done | bytes 8388624 | tf_op jit(solution)/shard_map/all_gather | solution.py:21
  93.7 31.7 %convolution_bitcast_fusion.1 = f32[512,128]{1,0:T(8,128)} fusion(f32[4,512,4096]{2,1,0:T(8,128)} %param.4, f32[4,4096,128]{2,1,0:T(8,128)} %all-gather.13.cloned.1.call-done), kind=kOutput, calls=%fused_computation.16 | convolution fusion | flops 12884901888 | bytes 42205184 | tf_op jit(solution)/shard_map/kmc,kcr->mr/dot_general | solution.py:16
  125.4 0.0 all-gather.25.cloned.1.call-update
  125.4 0.0 all-gather.15.cloned.1.call-start
  125.5 25.1 %all-gather.25.cloned.1.call-done = f32[2048,128]{1,0:T(8,128)} async-done(((f32[512,128]{1,0:T(8,128)}), f32[2048,128]{1,0:T(8,128)}) %all-gather.25.cloned.1.call-update) | async-done | bytes 1048592 | tf_op jit(solution)/shard_map/all_gather | solution.py:25
  150.6 1.3 reduce_sum.27
  151.9 0.7 bitcast_subtract_fusion.2
  152.6 0.0 all-gather.15.cloned.1.call-update
  152.7 0.0 all-gather.17.cloned.1.call-start
  152.7 29.3 %all-gather.15.cloned.1.call-done = f32[4096,128]{1,0:T(8,128)} async-done(((f32[512,128]{1,0:T(8,128)}), f32[4096,128]{1,0:T(8,128)}) %all-gather.15.cloned.1.call-update) | async-done | bytes 2097168 | tf_op jit(solution)/shard_map/all_gather | solution.py:29
  182.0 10.1 %fusion.18 = f32[128,512]{0,1:T(8,128)} fusion(f32[4096,128]{1,0:T(8,128)} %all-gather.15.cloned.1.call-done, f32[512,4096]{1,0:T(8,128)} %param.5), kind=kOutput, calls=%fused_computation.24 | convolution fusion | flops 3221225472 | bytes 10747904 | tf_op jit(solution)/shard_map/dot_general | solution.py:27
  192.0 0.0 all-gather.17.cloned.1.call-update
  192.0 0.0 all-gather.27.cloned.1.call-start
  192.1 4.5 slice_bitcast_fusion
  196.6 3.7 collective-permute-start
  200.3 5.9 %slice.30 = f32[3,4096,128]{2,1,0:T(8,128)} slice(f32[4,4096,128]{2,1,0:T(8,128)} %all-gather.13.cloned.1.call-done), slice={[0:3], [0:4096], [0:128]} | slice | bytes 12582912 | tf_op jit(solution)/shard_map/slice | solution.py:38
  206.2 39.4 %collective-permute-done = f32[4096,128]{1,0:T(8,128)S(1)} collective-permute-done((f32[4096,128]{1,0:T(8,128)}, f32[4096,128]{1,0:T(8,128)S(1)}, u32[]{:S(2)}, u32[]{:S(2)}) %collective-permute-start) | collective-permute-done | bytes 2097184 | tf_op jit(solution)/shard_map/ppermute | solution.py:12
  245.5 1.3 copy-done.3
  246.9 2.0 select_bitcast_fusion.1
  248.9 1.4 copy-done
  250.3 40.6 %fusion.12 = f32[512,128]{0,1:T(8,128)} fusion(f32[4,512,4096]{2,1,0:T(8,128)} %param.4, f32[3,4096,128]{2,1,0:T(8,128)S(1)} %copy-done, f32[1,4096,128]{2,1,0:T(8,128)S(1)} %select_bitcast_fusion.1), kind=kOutput, calls=%fused_computation.15 | convolution fusion | flops 12886999040 | bytes 42205184 | tf_op jit(solution)/shard_map/kmc,kcr->mr/dot_general | solution.py:16
  290.9 0.0 all-gather.19.cloned.1.call-start
  291.0 0.7 fusion.17
  291.7 0.8 copy.22
  292.6 25.3 %all-gather.27.cloned.1.call-done = f32[2048,128]{0,1:T(8,128)} async-done(((f32[512,128]{0,1:T(8,128)}), f32[2048,128]{0,1:T(8,128)}) %all-gather.27.cloned.1.call-update) | async-done | bytes 1048592 | tf_op jit(solution)/shard_map/all_gather | solution.py:25
  317.9 1.9 reshape.1
  319.8 0.6 reduce_sum.28
  320.4 1.7 bitcast_subtract_fusion.1
  322.1 0.0 all-gather.19.cloned.1.call-update
  322.2 0.0 all-gather.21.cloned.1.call-start
  322.2 29.3 %all-gather.19.cloned.1.call-done = f32[4096,128]{0,1:T(8,128)} async-done(((f32[512,128]{0,1:T(8,128)}), f32[4096,128]{0,1:T(8,128)}) %all-gather.19.cloned.1.call-update) | async-done | bytes 2097168 | tf_op jit(solution)/shard_map/all_gather | solution.py:29
  351.5 10.1 %fusion.19 = f32[128,512]{0,1:T(8,128)} fusion(f32[4096,128]{0,1:T(8,128)} %all-gather.19.cloned.1.call-done, f32[512,4096]{1,0:T(8,128)} %param.5), kind=kOutput, calls=%fused_computation.25 | convolution fusion | flops 3221225472 | bytes 10747904 | tf_op jit(solution)/shard_map/dot_general | solution.py:27
  361.6 0.0 all-gather.29.cloned.1.call-start
  361.6 4.7 collective-permute-start.1
  366.3 44.3 %collective-permute-done.1 = f32[4096,128]{1,0:T(8,128)} collective-permute-done((f32[4096,128]{1,0:T(8,128)}, f32[4096,128]{1,0:T(8,128)}, u32[]{:S(2)}, u32[]{:S(2)}) %collective-permute-start.1) | collective-permute-done | bytes 2097184 | tf_op jit(solution)/shard_map/ppermute | solution.py:12
  410.6 1.8 select_bitcast_fusion
  412.4 39.9 %fusion.9 = f32[512,128]{0,1:T(8,128)} fusion(f32[4,512,4096]{2,1,0:T(8,128)} %param.4, f32[3,4096,128]{2,1,0:T(8,128)} %slice.30, f32[1,4096,128]{2,1,0:T(8,128)S(1)} %select_bitcast_fusion.1, f32[1,4096,128]{2,1,0:T(8,128)S(1)} %select_bitcast_fusion), kind=kOutput, calls=%fused_computation.13 | convolution fusion | flops 12889096192 | bytes 44302336 | tf_op jit(solution)/shard_map/kmc,kcr->mr/dot_general | solution.py:16
  452.3 0.3 all-gather.23.cloned.1.call-start
  452.7 0.1 copy.23
  452.8 26.6 %all-gather.29.cloned.1.call-done = f32[2048,128]{0,1:T(8,128)} async-done(((f32[512,128]{0,1:T(8,128)}), f32[2048,128]{0,1:T(8,128)}) %all-gather.29.cloned.1.call-update) | async-done | bytes 1048592 | tf_op jit(solution)/shard_map/all_gather | solution.py:25
  479.4 1.9 reshape.2
  481.4 0.6 reduce_sum.29
  482.0 0.7 bitcast_subtract_fusion
  482.7 29.3 %all-gather.23.cloned.1.call-done = f32[4096,128]{0,1:T(8,128)} async-done(((f32[512,128]{0,1:T(8,128)}), f32[4096,128]{0,1:T(8,128)}) %all-gather.23.cloned.1.call-update) | async-done | bytes 2097168 | tf_op jit(solution)/shard_map/all_gather | solution.py:29
  512.1 9.4 %convolution_bitcast_fusion = f32[1,512,128]{2,1,0:T(8,128)S(1)} fusion(f32[4096,128]{0,1:T(8,128)} %all-gather.23.cloned.1.call-done, f32[512,4096]{1,0:T(8,128)} %param.5), kind=kOutput, calls=%fused_computation.14 | convolution fusion | flops 3221225472 | bytes 10747904 | tf_op jit(solution)/shard_map/dot_general | solution.py:27
  521.5 0.9 pad_maximum_fusion.1
  (17 shorter events, 0.1 us)
Async XLA Ops:
  6.5 87.2 %all-gather.13.cloned.1.call-start = ((), (), s32[]{:S(2)}) async-start(), calls=%async_computation | async-start | bytes 9437184 | tf_op jit(solution)/shard_map/all_gather | solution.py:21
  7.3 144.6 %copy-start.5 = (f32[3,512,128]{2,1,0:T(8,128)S(1)}, f32[3,512,128]{2,1,0:T(8,128)}, u32[]{:S(2)}) copy-start(f32[3,512,128]{2,1,0:T(8,128)} %param.6) | copy-start | bytes 2359300
  7.3 143.3 %all-gather.25.cloned.1.call-start = ((), (), s32[]{:S(2)}) async-start(), calls=%async_computation.6 | async-start | bytes 1310720 | tf_op jit(solution)/shard_map/all_gather | solution.py:25
  125.4 56.5 %all-gather.15.cloned.1.call-start = ((), (), s32[]{:S(2)}) async-start(), calls=%async_computation.1 | async-start | bytes 2359296 | tf_op jit(solution)/shard_map/all_gather | solution.py:29
  152.7 94.2 %all-gather.17.cloned.1.call-start = ((), (), s32[]{:S(2)}) async-start(), calls=%async_computation.2 | async-start | bytes 2359296 | tf_op jit(solution)/shard_map/all_gather | solution.py:35
  192.0 125.8 %all-gather.27.cloned.1.call-start = ((), (), s32[]{:S(2)}) async-start(), calls=%async_computation.7 | async-start | bytes 1310720 | tf_op jit(solution)/shard_map/all_gather | solution.py:25
  196.6 48.9 %collective-permute-start = (f32[4096,128]{1,0:T(8,128)}, f32[4096,128]{1,0:T(8,128)S(1)}, u32[]{:S(2)}, u32[]{:S(2)}) collective-permute-start(f32[4096,128]{1,0:T(8,128)} %get-tuple-element.6), channel_id=1, source_target_pairs={{0,8},{8,16},{16,24},{1,9},{9,17},{17,25},{2,10},{10,18},{18,26},{... | collective-permute-start | bytes 6291464 | tf_op jit(solution)/shard_map/ppermute | solution.py:12
  245.5 1.3 copy-start.3
  246.9 3.4 copy-start
  290.9 60.5 %all-gather.19.cloned.1.call-start = ((), (), s32[]{:S(2)}) async-start(), calls=%async_computation.3 | async-start | bytes 2359296 | tf_op jit(solution)/shard_map/all_gather | solution.py:29
  322.2 88.4 %all-gather.21.cloned.1.call-start = ((), (), s32[]{:S(2)}) async-start(), calls=%async_computation.4 | async-start | bytes 2359296 | tf_op jit(solution)/shard_map/all_gather | solution.py:35
  361.6 117.8 %all-gather.29.cloned.1.call-start = ((), (), s32[]{:S(2)}) async-start(), calls=%async_computation.8 | async-start | bytes 1310720 | tf_op jit(solution)/shard_map/all_gather | solution.py:25
  361.6 49.0 %collective-permute-start.1 = (f32[4096,128]{1,0:T(8,128)}, f32[4096,128]{1,0:T(8,128)}, u32[]{:S(2)}, u32[]{:S(2)}) collective-permute-start(f32[4096,128]{1,0:T(8,128)} %get-tuple-element.5), channel_id=1, source_target_pairs={{0,8},{8,16},{16,24},{1,9},{9,17},{17,25},{2,10},{10,18},{18,26},{... | collective-permute-start | bytes 6291464 | tf_op jit(solution)/shard_map/ppermute | solution.py:12
  412.4 40.3 %copy-start.4 = (f32[1,512,128]{2,1,0:T(8,128)S(1)}, f32[1,512,128]{2,1,0:T(8,128)}, u32[]{:S(2)}) copy-start(f32[1,512,128]{2,1,0:T(8,128)} %get-tuple-element.7) | copy-start | bytes 786436
  452.3 59.7 %all-gather.23.cloned.1.call-start = ((), (), s32[]{:S(2)}) async-start(), calls=%async_computation.5 | async-start | bytes 2359296 | tf_op jit(solution)/shard_map/all_gather | solution.py:29
  481.3 40.1 %copy-start.1 = (f32[128,512]{0,1:T(8,128)S(1)}, f32[128,512]{0,1:T(8,128)}, u32[]{:S(2)}) copy-start(f32[128,512]{0,1:T(8,128)} %fusion.18) | copy-start | bytes 786436
  481.4 40.1 %copy-start.2 = (f32[128,512]{0,1:T(8,128)S(1)}, f32[128,512]{0,1:T(8,128)}, u32[]{:S(2)}) copy-start(f32[128,512]{0,1:T(8,128)} %fusion.19) | copy-start | bytes 786436
Sparse Core Ops, SparseCore 0:
  8.9 84.7 all-gather.12
  125.6 24.9 all-gather.24
  152.8 29.1 all-gather.14
  192.2 28.5 all-gather.16
  291.1 26.7 all-gather.26
  322.3 29.1 all-gather.18
  361.7 28.5 all-gather.20
  452.5 26.8 all-gather.28
  482.9 29.1 all-gather.22
